TPU v7x, 32 devices: a whole 2x2x4 slice. The times are simulated.
32 devices in a mesh: ctx: 8 (over y, x, core), grp: 4 (over z).
Axes of the slice: x: 2, y: 2, z: 4, core: 2. Of those that a mesh axis runs over, the one named last changes fastest.
Arguments:
- query_in: bfloat16 [8192, 4096], P('ctx', 'grp'), may hold values from -6 to 6
- key_in: bfloat16 [8192, 4096], P('ctx', 'grp'), may hold values from -6 to 6
- value_in: bfloat16 [8192, 4096], P('ctx', 'grp'), may hold values from -6 to 6
- residues: float32 [256, 16], P('grp'), may hold values from -1.5 to 1.5
- decay_time: float32 [256, 16], P('grp'), may hold values from 20 to 32768
- skip_gain: float32 [4096], P('grp'), may hold values from 0.5 to 1.5
- out_proj: bfloat16 [4096, 4096], P('ctx', 'grp'), may hold values from -0.09375 to 0.09375
- doc_lengths: int32 [4], replicated, may hold values from 1 to 4096, 8192 in all
- grad_out: bfloat16 [8192, 4096], P('ctx', 'grp'), may hold values from -6 to 6
Outputs:
- mixed_out: bfloat16 [8192, 4096], P('ctx', 'grp')
- grad_query: bfloat16 [8192, 4096], P('ctx', 'grp')
- grad_key: bfloat16 [8192, 4096], P('ctx', 'grp')
- grad_value: bfloat16 [8192, 4096], P('ctx', 'grp')
- grad_proj: float32 [4096, 4096], P('ctx', 'grp')
Inputs may be any that keep to these rules, and one draw needn't show every extreme that they name: `doc_lengths`: document lengths in window order, summing to 8192; the longest is exactly 4096.
All inputs are finite; a program needn't handle non-finite values.
Results may differ from a plain program's by a relative error of at most 0.013.
Values may be sent and summed in bfloat16 or wider, within the bound.
A program may use at most 192 MiB of HBM per device.

v0:
```python
import jax
import jax.numpy as jnp
from jax import lax
from jax.sharding import PartitionSpec as P


def prefix(value, axis, combine, identity, reverse):
    size, position = (lax.axis_size(axis), lax.axis_index(axis))
    everything = jax.tree.map(
        lambda part, kind: lax.all_gather(part.astype(kind), axis),
        value,
        jax.tree.map(lambda a: jnp.bfloat16 if a.dtype == jnp.float32 else a.dtype, value),
    )
    start = jax.tree.map(
        lambda part, zero: jnp.broadcast_to(jnp.asarray(zero, part.dtype), part.shape),
        value,
        identity,
    )

    def step(k, before):
        at = size - 1 - k if reverse else k
        reached = at > position if reverse else at < position
        new = combine(
            before, jax.tree.map(lambda part, own: part[at].astype(own.dtype), everything, value)
        )
        return jax.tree.map(lambda a, b: jnp.where(reached, a, b), new, before)

    return lax.fori_loop(0, size, step, start)


def chain(former, latter):
    return (former[0] * latter[0], latter[0][:, None, :] * former[1] + latter[1])


def doc_index(starts, where_now):
    return jnp.sum((starts[None, :] <= where_now[:, None]).astype(jnp.int32), axis=1) - 1


def local(
    query_in, key_in, value_in, residues, decay_time, skip_gain, out_proj, doc_lengths, grad_out
):
    tok_rows, channels = query_in.shape
    filters, poles = residues.shape
    members = channels // filters
    block_len = min(128, tok_rows)
    block_count = tok_rows // block_len
    starts = jnp.cumsum(doc_lengths) - doc_lengths
    where_now = lax.axis_index("ctx") * tok_rows + jnp.arange(tok_rows, dtype=jnp.int32)
    doc_ids = doc_index(starts, where_now).reshape(block_count, block_len)
    prior_ids = doc_index(starts, where_now - 1).reshape(block_count, block_len)[:, 0]
    decay_rate = 1.0 / decay_time
    residue_scaled = residues * jnp.sqrt(-jnp.expm1(-2.0 * decay_rate))
    lag_steps = jnp.arange(block_len, dtype=jnp.float32)
    powers = jnp.exp(-lag_steps[None, None, :] * decay_rate[:, :, None])
    lagged = jnp.sum(residue_scaled[:, :, None] * powers, axis=1)
    positions = jnp.arange(block_len, dtype=jnp.int32)
    lag_index = jnp.clip(positions[:, None] - positions[None, :], 0, block_len - 1)
    toeplitz = jnp.take(lagged, lag_index, axis=1)
    causal = positions[:, None] >= positions[None, :]
    same_docs = (doc_ids[:, :, None] == doc_ids[:, None, :]) & causal[None]
    masked = toeplitz[None] * same_docs[:, None].astype(jnp.float32)
    step_enter = jnp.exp(-(lag_steps + 1.0)[None, None, :] * decay_rate[:, :, None])
    alive_enter = (doc_ids == prior_ids[:, None]).astype(jnp.float32)
    enter_gain = residue_scaled[None, :, :, None] * step_enter[None] * alive_enter[:, None, None, :]
    step_leave = jnp.exp(-(block_len - 1.0 - lag_steps)[None, None, :] * decay_rate[:, :, None])
    alive_leave = (doc_ids == doc_ids[:, -1:]).astype(jnp.float32)
    leave_gain = step_leave[None] * alive_leave[:, None, None, :]
    across_gain = (
        jnp.exp(-block_len * decay_rate)[None]
        * (prior_ids == doc_ids[:, -1]).astype(jnp.float32)[:, None, None]
    )
    unit_decay = jnp.ones((filters, poles), jnp.float32)
    empty_state = jnp.zeros((filters, members, poles), jnp.float32)
    highest = lax.Precision.HIGHEST
    query_f = query_in.astype(jnp.float32)
    key_f = key_in.astype(jnp.float32)
    value_f = value_in.astype(jnp.float32)
    product_f = (key_f * value_f).astype(jnp.bfloat16).astype(jnp.float32)
    gathered = lax.all_gather(out_proj, "ctx", axis=0, tiled=True)
    shaped = product_f.reshape(block_count, block_len, filters, members)
    within = jnp.einsum("bgts,bsgc->btgc", masked, shaped, precision=highest)
    block_state = jnp.einsum("bgns,bsgc->bgcn", leave_gain, shaped, precision=highest)
    summary = (unit_decay, empty_state)
    for number in range(block_count):
        summary = chain(summary, (across_gain[number], block_state[number]))
    incoming = prefix(summary, "ctx", chain, (unit_decay, empty_state), False)[1]
    entering = []
    for number in range(block_count):
        entering.append(incoming)
        incoming = across_gain[number][:, None, :] * incoming + block_state[number]
    beyond = jnp.einsum("bgnt,bgcn->btgc", enter_gain, jnp.stack(entering), precision=highest)
    convolved = (within + beyond).reshape(tok_rows, channels)
    grad_full = lax.all_gather(grad_out, "grp", axis=1, tiled=True)
    grad_gated = jnp.dot(grad_full, gathered, preferred_element_type=jnp.float32)
    grad_filtered = grad_gated * query_f
    shaped = grad_filtered.reshape(block_count, block_len, filters, members)
    within = jnp.einsum("bgts,btgc->bsgc", masked, shaped, precision=highest)
    block_adjoint = jnp.einsum("bgnt,btgc->bgcn", enter_gain, shaped, precision=highest)
    summary = (unit_decay, empty_state)
    for number in reversed(range(block_count)):
        summary = chain(summary, (across_gain[number], block_adjoint[number]))
    incoming = prefix(summary, "ctx", chain, (unit_decay, empty_state), True)[1]
    leaving = [None] * block_count
    for number in reversed(range(block_count)):
        leaving[number] = incoming
        incoming = block_adjoint[number] + across_gain[number][:, None, :] * incoming
    beyond = jnp.einsum("bgns,bgcn->bsgc", leave_gain, jnp.stack(leaving), precision=highest)
    grad_product = (within + beyond).reshape(tok_rows, channels) + skip_gain * grad_filtered
    grad_full, grad_gated, grad_product = (grad_full, grad_gated, grad_product)
    filtered = convolved + skip_gain * product_f
    gated = (query_f * filtered).astype(jnp.bfloat16)
    partial_value = lax.dot_general(
        gated, gathered, (((1,), (1,)), ((), ())), preferred_element_type=jnp.float32
    )
    rounded = lax.optimization_barrier(partial_value.astype(jnp.bfloat16)).astype(jnp.float32)
    mixed_out = lax.psum_scatter(
        rounded.astype(jnp.bfloat16), "grp", scatter_dimension=1, tiled=True
    )
    grad_query = (grad_gated * filtered).astype(jnp.bfloat16)
    grad_key = (grad_product * value_f).astype(jnp.bfloat16)
    grad_value = (grad_product * key_f).astype(jnp.bfloat16)
    term_whole = lax.dot_general(
        grad_full, gated, (((0,), (0,)), ((), ())), preferred_element_type=jnp.float32
    )
    grad_proj = lax.psum_scatter(
        term_whole.astype(jnp.bfloat16), "ctx", scatter_dimension=0, tiled=True
    ).astype(jnp.float32)
    return (mixed_out, grad_query, grad_key, grad_value, grad_proj)


def solution(mesh):
    return jax.shard_map(
        local,
        mesh=mesh,
        in_specs=(
            P("ctx", "grp"),
            P("ctx", "grp"),
            P("ctx", "grp"),
            P("grp", None),
            P("grp", None),
            P("grp"),
            P("ctx", "grp"),
            P(),
            P("ctx", "grp"),
        ),
        out_specs=(
            P("ctx", "grp"),
            P("ctx", "grp"),
            P("ctx", "grp"),
            P("ctx", "grp"),
            P("ctx", "grp"),
        ),
        check_vma=False,
    )
```

profile of v0, /device:TPU:0, one launch (start us, length us, event | category | flops | bytes accessed | tf_op | source)
XLA Modules:
  0.0 472.9 jit_solution(16849011690872754440)
XLA Ops:
  11.7 3.9 fusion.20
  15.6 3.9 copy.180
  26.9 3.4 fusion.16
  35.3 10.7 %all_gather.22 = bf16[8,64,16]{1,2,0:T(8,128)(2,1)S(1)} all-gather(bf16[1,64,16]{1,2,0:T(8,128)(2,1)} %get-tuple-element.365), channel_id=1, replica_groups=mesh['ctx'=8,'grp'=4] {'ctx'}, dimensions={0}, use_global_device_ids=true | all-gather | bytes 18432 | tf_op jit(solution)/shard_map/all_gather | solution.py:10
  46.0 9.9 %all_gather.23 = bf16[8,64,16,16]{1,3,2,0:T(8,128)(2,1)S(1)} all-gather(bf16[1,64,16,16]{1,3,2,0:T(8,128)(2,1)} %copy.195), channel_id=1, replica_groups=mesh['ctx'=8,'grp'=4] {'ctx'}, dimensions={0}, use_global_device_ids=true | all-gather | bytes 294912 | tf_op jit(solution)/shard_map/all_gather | solution.py:10
  58.6 54.4 %gather_fusion = f32[16384,64]{1,0:T(8,128)} fusion(f32[64,128]{0,1:T(8,128)S(1)} %copy.183, s32[16384]{0:T(1024)S(1)} %fusion.41), kind=kCustom, calls=%fused_computation | custom fusion | bytes 8454144 | tf_op jit(solution)/shard_map/jit(_take)/gather | solution.py:58
  113.0 10.0 %select_bitcast_fusion = f32[64,128,128]{0,2,1:T(8,128)} fusion(f32[128,128,64]{2,1,0:T(8,128)} %bitcast.199, pred[128,128]{1,0:T(8,128)(4,1)S(1)} %fusion.44), kind=kLoop, calls=%fused_computation.15 | loop fusion | flops 1048576 | bytes 8404992 | tf_op jit(solution)/shard_map/jit(_take)/select_n | solution.py:58
  123.0 7.3 %copy.184 = f32[64,128,128]{2,1,0:T(8,128)} copy(f32[64,128,128]{0,2,1:T(8,128)} %select_bitcast_fusion) | data formatting | bytes 8388608 | tf_op jit(solution)/shard_map/jit(_take)/select_n | solution.py:58
  134.1 5.2 %fusion.12 = f32[8,64,16,128]{3,2,1,0:T(8,128)S(1)} fusion(f32[8,64,16,16]{3,2,1,0:T(8,128)S(1)} %bitcast_dynamic-update-slice_fusion.8, f32[8,128]{1,0:T(8,128)S(1)} %get-tuple-element.379, f32[64,16,128]{2,1,0:T(8,128)S(1)} %get-tuple-element.369), kind=kOutput, calls=%fused_computation.20 | convolution fusion | flops 202375168 | bytes 5246976 | tf_op jit(solution)/shard_map/bgnt,bgcn->btgc/dot_general | solution.py:91
  139.3 26.9 %add_bitcast_fusion.1 = f32[8,128,64,16]{1,3,2,0:T(8,128)S(1)} fusion(f32[8,64,16,128]{3,2,1,0:T(8,128)S(1)} %fusion.12, f32[8,128,128]{2,1,0:T(8,128)S(1)} %and_convert_fusion, f32[64,128,128]{2,1,0:T(8,128)S(1)} %copy-done, bf16[8,128,64,16]{1,0,3,2:T(8,128)(2,1)S(1)} %bitcast.198), kind=kOutput, calls=%fused_computation.41 | convolution fusion | flops 1620049920 | bytes 15204352 | tf_op jit(solution)/shard_map/bgts,bsgc->btgc/dot_general | solution.py:81
  171.6 5.5 %copy.206 = f32[1024,1024]{1,0:T(8,128)} copy(f32[1024,1024]{0,1:T(8,128)} %bitcast.201) | data formatting | bytes 8388608 | tf_op jit(solution)/shard_map/reshape | solution.py:92
  177.2 39.3 %all-gather.3.cloned.1.call-done = bf16[4096,1024]{1,0:T(8,128)(2,1)} async-done(((bf16[512,1024]{1,0:T(8,128)(2,1)}), bf16[4096,1024]{1,0:T(8,128)(2,1)}) %all-gather.3.cloned.1.call-update) | async-done | bytes 8388624 | tf_op jit(solution)/shard_map/all_gather | solution.py:79
  216.5 17.4 %multiply_convert_fusion = (bf16[1024,1024]{1,0:T(8,128)(2,1)}, bf16[1024,1024]{1,0:T(8,128)(2,1)S(1)}, f32[1024,1024]{1,0:T(8,128)}) fusion(f32[1024,1024]{1,0:T(8,128)} %copy.206, bf16[1024,1024]{1,0:T(8,128)(2,1)S(1)} %copy-done.9, f32[1024]{0:T(1024)S(1)} %copy-done.17, bf16[1024,1024]{1,0:T(8,128)(2,1)} %param.13, ...), kind=kOutput, calls=%fused_computation.39 | convolution fusion | flops 8599371776 | bytes 33558528 | tf_op jit(solution)/shard_map/dot_general | solution.py:94
  235.2 11.4 %convert_bitcast_fusion = bf16[4096,1024]{0,1:T(8,128)(2,1)} fusion(bf16[1024,1024]{1,0:T(8,128)(2,1)S(1)} %get-tuple-element.359, bf16[1024,4096]{1,0:T(8,128)(2,1)S(1)} %copy-done.18), kind=kOutput, calls=%fused_computation.16 | convolution fusion | flops 8594128896 | bytes 18874368 | tf_op jit(solution)/shard_map/dot_general | solution.py:122
  248.2 14.5 %convolution_convert_fusion = bf16[1024,4096]{1,0:T(8,128)(2,1)} fusion(bf16[1024,1024]{1,0:T(8,128)(2,1)S(1)} %copy-done.21, bf16[4096,1024]{1,0:T(8,128)(2,1)} %all-gather.3.cloned.1.call-done), kind=kOutput, calls=%fused_computation.17 | convolution fusion | flops 8594128896 | bytes 18874368 | tf_op jit(solution)/shard_map/dot_general | solution.py:112
  263.4 9.0 %all_gather.26 = bf16[8,64,16]{1,2,0:T(8,128)(2,1)S(1)} all-gather(bf16[1,64,16]{1,2,0:T(8,128)(2,1)S(1)} %get-tuple-element.363), channel_id=1, replica_groups=mesh['ctx'=8,'grp'=4] {'ctx'}, dimensions={0}, use_global_device_ids=true | all-gather | bytes 18432 | tf_op jit(solution)/shard_map/all_gather | solution.py:10
  272.4 5.3 %copy.207 = f32[1024,1024]{0,1:T(8,128)} copy(f32[1024,1024]{1,0:T(8,128)} %get-tuple-element.360) | data formatting | bytes 8388608 | tf_op jit(solution)/shard_map/mul | solution.py:95
  281.2 7.0 %fusion.10 = f32[8,64,16,16]{3,2,1,0:T(8,128)S(1)} fusion(f32[8,128,64,16]{1,0,3,2:T(8,128)S(1)} %bitcast.195, f32[8,128]{1,0:T(8,128)S(1)} %get-tuple-element.379, f32[64,16,128]{2,1,0:T(8,128)S(1)} %get-tuple-element.369), kind=kOutput, calls=%fused_computation.18 | convolution fusion | flops 202375168 | bytes 5246976 | tf_op jit(solution)/shard_map/bgnt,btgc->bgcn/dot_general | solution.py:98
  290.9 10.2 %all_gather.27 = bf16[8,64,16,16]{1,3,2,0:T(8,128)(2,1)S(1)} all-gather(bf16[1,64,16,16]{1,3,2,0:T(8,128)(2,1)S(1)} %copy.213), channel_id=1, replica_groups=mesh['ctx'=8,'grp'=4] {'ctx'}, dimensions={0}, use_global_device_ids=true | all-gather | bytes 294912 | tf_op jit(solution)/shard_map/all_gather | solution.py:10
  309.4 29.0 %fusion.2 = f32[8,64,16,128]{3,2,1,0:T(8,128)S(1)} fusion(f32[8,128,128]{2,1,0:T(8,128)S(1)} %copy-done.11, f32[64,128,128]{2,1,0:T(8,128)S(1)} %copy-done.1, f32[8,128,64,16]{1,0,3,2:T(8,128)S(1)} %bitcast.196), kind=kOutput, calls=%fused_computation.7 | convolution fusion | flops 1619001344 | bytes 13107200 | tf_op jit(solution)/shard_map/bgts,btgc->bsgc/dot_general | solution.py:97
  338.4 5.0 %add_bitcast_fusion = f32[8,128,64,16]{1,3,2,0:T(8,128)S(1)} fusion(f32[8,64,16,128]{3,2,1,0:T(8,128)S(1)} %fusion.2, f32[8,64,16,16]{3,2,1,0:T(8,128)S(1)} %bitcast_dynamic-update-slice_fusion, f32[8,128]{1,0:T(8,128)S(1)} %get-tuple-element.380, f32[64,16,128]{2,1,0:T(8,128)S(1)} %copy-done.13), kind=kOutput, calls=%fused_computation.38 | convolution fusion | flops 203423744 | bytes 9441280 | tf_op jit(solution)/shard_map/bgns,bgcn->bsgc/dot_general | solution.py:107
  348.8 5.5 %copy.217 = f32[1024,1024]{1,0:T(8,128)} copy(f32[1024,1024]{0,1:T(8,128)} %bitcast.203) | data formatting | bytes 8388608 | tf_op jit(solution)/shard_map/reshape | solution.py:108
  354.3 7.8 %fusion.19 = (bf16[1024,1024]{1,0:T(8,128)(2,1)}, bf16[1024,1024]{1,0:T(8,128)(2,1)}) fusion(bf16[1024,1024]{1,0:T(8,128)(2,1)} %param.14, f32[1024,1024]{1,0:T(8,128)} %copy.217, f32[1024,1024]{1,0:T(8,128)} %get-tuple-element.360, f32[1024]{0:T(1024)S(1)} %copy-done.17, bf16[1024,1024]{1,0:T(8,128)(2,1)S(1)} %copy-done.8), kind=kLoop, calls=%fused_computation.32 | loop fusion | flops 8388608 | bytes 16781312 | tf_op jit(solution)/shard_map/convert_element_type | solution.py:121
  364.7 101.5 %reduce-scatter.3.cloned.1.call-done = bf16[1024,1024]{1,0:T(8,128)(2,1)} async-done(((bf16[1024,4096]{1,0:T(8,128)(2,1)}), bf16[1024,1024]{1,0:T(8,128)(2,1)}) %reduce-scatter.3.cloned.1.call-update) | async-done | bytes 2097168 | tf_op jit(solution)/shard_map/reduce_scatter | solution.py:116
  (154 shorter events, 55.6 us)
Async XLA Ops:
  7.2 4.5 copy-start.7
  7.2 170.0 %all-gather.5.cloned.1.call-start = ((), (), s32[]{:S(2)}) async-start(), calls=%async_computation.4 | async-start | bytes 10485760 | tf_op jit(solution)/shard_map/all_gather | solution.py:93
  7.9 208.5 %all-gather.3.cloned.1.call-start = ((), (), s32[]{:S(2)}) async-start(), calls=%async_computation.2 | async-start | bytes 9437184 | tf_op jit(solution)/shard_map/all_gather | solution.py:79
  8.7 353.4 %reduce-scatter.5.cloned.1.call-start = ((), (), s32[]{:S(2)}) async-start(), calls=%async_computation.5 | async-start | bytes 9437184 | tf_op jit(solution)/shard_map/reduce_scatter | solution.py:125
  15.6 6.5 %copy-start.19 = (s32[4]{0:T(128)S(1)}, s32[4]{0:T(128)}, u32[]{:S(2)}) copy-start(s32[4]{0:T(128)} %param.20) | copy-start | bytes 52
  25.0 8.5 %copy-start.14 = (f32[64,16]{1,0:T(8,128)}, f32[64,16]{1,0:T(8,128)S(1)}, u32[]{:S(2)}) copy-start(f32[64,16]{1,0:T(8,128)S(1)} %copy.186) | copy-start | bytes 12292
  26.9 6.6 %copy-start.12 = (f32[64,16,128]{2,1,0:T(8,128)}, f32[64,16,128]{2,1,0:T(8,128)S(1)}, u32[]{:S(2)}) copy-start(f32[64,16,128]{2,1,0:T(8,128)S(1)} %get-tuple-element.375) | copy-start | bytes 1572868
  30.3 2.1 copy-start.3
  130.3 3.1 copy-start.4
  130.6 8.7 %copy-start.10 = (f32[8,128,128]{2,1,0:T(8,128)}, f32[8,128,128]{2,1,0:T(8,128)S(1)}, u32[]{:S(2)}) copy-start(f32[8,128,128]{2,1,0:T(8,128)S(1)} %and_convert_fusion) | copy-start | bytes 1572868
  134.1 5.2 %copy-start = (f32[64,128,128]{2,1,0:T(8,128)S(1)}, f32[64,128,128]{2,1,0:T(8,128)}, u32[]{:S(2)}) copy-start(f32[64,128,128]{2,1,0:T(8,128)} %copy.184) | copy-start | bytes 12582916
  171.6 44.8 %copy-start.9 = (bf16[1024,1024]{1,0:T(8,128)(2,1)S(1)}, bf16[1024,1024]{1,0:T(8,128)(2,1)}, u32[]{:S(2)}) copy-start(bf16[1024,1024]{1,0:T(8,128)(2,1)} %fusion.20) | copy-start | bytes 6291460
  171.6 44.8 %copy-start.17 = (f32[1024]{0:T(1024)S(1)}, f32[1024]{0:T(1024)}, u32[]{:S(2)}) copy-start(f32[1024]{0:T(1024)} %param.18) | copy-start | bytes 12292
  216.5 18.8 %copy-start.18 = (bf16[1024,4096]{1,0:T(8,128)(2,1)S(1)}, bf16[1024,4096]{1,0:T(8,128)(2,1)}, u32[]{:S(2)}) copy-start(bf16[1024,4096]{1,0:T(8,128)(2,1)} %all-gather.5.cloned.1.call-done) | copy-start | bytes 25165828
  246.6 1.6 copy-start.21
  246.6 219.5 %reduce-scatter.3.cloned.1.call-start = ((), (), s32[]{:S(2)}) async-start(), calls=%async_computation.3 | async-start | bytes 10485760 | tf_op jit(solution)/shard_map/reduce_scatter | solution.py:116
  281.2 7.0 %copy-start.5 = (f32[128,8,8,128]{3,2,1,0:T(8,128)}, f32[128,8,8,128]{3,2,1,0:T(8,128)S(1)}, u32[]{:S(2)}) copy-start(f32[128,8,8,128]{3,2,1,0:T(8,128)S(1)} %copy.221) | copy-start | bytes 12582916
  288.2 2.0 copy-start.2
  290.2 11.9 %copy-start.15 = (f32[64,16]{1,0:T(8,128)S(1)}, f32[64,16]{1,0:T(8,128)}, u32[]{:S(2)}) copy-start(f32[64,16]{1,0:T(8,128)} %copy-done.14) | copy-start | bytes 12292
  304.9 4.5 copy-start.1
  304.9 4.5 copy-start.6
  304.9 4.5 copy-start.11
  309.4 29.0 %copy-start.13 = (f32[64,16,128]{2,1,0:T(8,128)S(1)}, f32[64,16,128]{2,1,0:T(8,128)}, u32[]{:S(2)}) copy-start(f32[64,16,128]{2,1,0:T(8,128)} %copy-done.12) | copy-start | bytes 1572868
  348.8 5.5 %copy-start.8 = (bf16[1024,1024]{1,0:T(8,128)(2,1)S(1)}, bf16[1024,1024]{1,0:T(8,128)(2,1)}, u32[]{:S(2)}) copy-start(bf16[1024,1024]{1,0:T(8,128)(2,1)} %param.15) | copy-start | bytes 6291460
  (2 other events, 2.0 us)
Sparse Core Ops, SparseCore 0:
  9.6 152.3 all-gather.4
  163.8 52.5 all-gather.2
  246.8 71.9 reduce-scatter.4
  321.7 144.4 reduce-scatter.2
where the time goes:
time: 480 us; the launch traced here: 473 us
  waiting for transfers between devices  142 us (30%)
  matrix products  120 us (25%)
  local copies, waits for them, and re-layouts  116 us (24%)
  other arithmetic  39.7 us (8%)
  blocking collectives  39.7 us (8%)
  between operations  14.4 us (3%)
    reduce_scatter x1, waiting for transfers between devices, local(): lax.psum_scatter(rounded.astype(jnp.bfloat16), 'grp', scatter_dimension=1...  101 us
    gather x1, local copies, waits for them, and re-layouts, local(): toeplitz = jnp.take(lagged, lag_index, axis=1)  54.4 us
    all_gather x4, blocking collectives, prefix(): lax.all_gather(part.astype(kind), axis)  39.7 us
    all_gather x1, waiting for transfers between devices, local(): gathered = lax.all_gather(out_proj, 'ctx', axis=0, tiled=True)  39.3 us
    dot_general x1, matrix products, local(): within = jnp.einsum('bgts,btgc->bsgc', masked, shaped, precision=highest)  29 us
    dot_general x1, matrix products, local(): within = jnp.einsum('bgts,bsgc->btgc', masked, shaped, precision=highest)  26.9 us
    unnamed x53, local copies, waits for them, and re-layouts  22.2 us
    dot_general x1, matrix products, local(): jnp.dot(grad_full, gathered, preferred_element_type=jnp.float32)  17.4 us
  transfers between devices with their start and end apart: 4, of which 2 were waited for; matrix products, arithmetic and copies ran while one was open for 51% of the time, Pallas kernels for 0%

commit v1 on v0

--- a/solution.py
+++ b/solution.py
@@ -76,7 +76,12 @@
     key_f = key_in.astype(jnp.float32)
     value_f = value_in.astype(jnp.float32)
     product_f = (key_f * value_f).astype(jnp.bfloat16).astype(jnp.float32)
-    gathered = lax.all_gather(out_proj, "ctx", axis=0, tiled=True)
+    ring = [out_proj]
+    for hop in range(7):
+        ring.append(lax.ppermute(ring[-1], "ctx", [(dev, (dev + 1) % 8) for dev in range(8)]))
+    gathered = jnp.roll(
+        jnp.concatenate(ring[::-1], axis=0), (lax.axis_index("ctx") + 1) * ring[0].shape[0], axis=0
+    )
     shaped = product_f.reshape(block_count, block_len, filters, members)
     within = jnp.einsum("bgts,bsgc->btgc", masked, shaped, precision=highest)
     block_state = jnp.einsum("bgns,bsgc->bgcn", leave_gain, shaped, precision=highest)

time: 480 us -> 615 us (1.28)
  waiting for transfers between devices: 142 us -> 228 us
  local copies, waits for them, and re-layouts: 116 us -> 145 us
  other arithmetic: 39.7 us -> 55.7 us
    unnamed x53 -> x120, local copies, waits for them, and re-layouts: 22.2 us -> 67.7 us
    reduce_scatter x1, waiting for transfers between devices: 0.01 us -> 45 us  [local(): lax.psum_scatter(term_whole.astype(jnp.bfloat16), 'ctx', scatter_dimensio...]
    reduce_scatter x1, waiting for transfers between devices: 101 us -> 145 us  [local(): lax.psum_scatter(rounded.astype(jnp.bfloat16), 'grp', scatter_dimension=1...]
    all_gather x1 -> x0, waiting for transfers between devices: 39.3 us -> none  [local(): gathered = lax.all_gather(out_proj, 'ctx', axis=0, tiled=True)]
    ppermute x0 -> x7, waiting for transfers between devices: none -> 37 us  [local(): lax.ppermute(ring[-1], 'ctx', [(dev, (dev + 1) % 8) for dev in range(8)])]
    reshape x2 -> x0, local copies, waits for them, and re-layouts: 11 us -> none  [the longest x1 5.53 us: local(): convolved = (within + beyond).reshape(tok_rows, channels)]
    unnamed x12, other arithmetic: 10.2 us -> 17.5 us
    select_n x16, other arithmetic: 0.93 us -> 7.65 us  [step(): return jax.tree.map(lambda a, b: jnp.where(reached, a, b), new, before)]
  transfers between devices with their start and end apart: 4 -> 10, of which waited for: 2 -> 6; matrix products, arithmetic and copies ran while one was open for 51% -> 28% of each run, Pallas kernels for 0% -> 0%
where the time goes in v1:
time: 615 us; the launch traced here: 604 us
  waiting for transfers between devices  228 us (37%)
  local copies, waits for them, and re-layouts  145 us (24%)
  matrix products  118 us (19%)
  other arithmetic  55.7 us (9%)
  blocking collectives  40.6 us (7%)
  between operations  14.6 us (2%)
    reduce_scatter x1, waiting for transfers between devices, local(): lax.psum_scatter(rounded.astype(jnp.bfloat16), 'grp', scatter_dimension=1...  145 us
    unnamed x120, local copies, waits for them, and re-layouts  67.7 us
    gather x1, local copies, waits for them, and re-layouts, local(): toeplitz = jnp.take(lagged, lag_index, axis=1)  54.4 us
    reduce_scatter x1, waiting for transfers between devices, local(): lax.psum_scatter(term_whole.astype(jnp.bfloat16), 'ctx', scatter_dimensio...  45 us
    all_gather x4, blocking collectives, prefix(): lax.all_gather(part.astype(kind), axis)  40.6 us
    ppermute x7, waiting for transfers between devices, local(): lax.ppermute(ring[-1], 'ctx', [(dev, (dev + 1) % 8) for dev in range(8)])  37 us
    dot_general x1, matrix products, local(): within = jnp.einsum('bgts,btgc->bsgc', masked, shaped, precision=highest)  28.8 us
    dot_general x1, matrix products, local(): within = jnp.einsum('bgts,bsgc->btgc', masked, shaped, precision=highest)  26.4 us
  transfers between devices with their start and end apart: 10, of which 6 were waited for; matrix products, arithmetic and copies ran while one was open for 28% of the time, Pallas kernels for 0%

profile of v1, /device:TPU:0, one launch (start us, length us, event | category | flops | bytes accessed | tf_op | source)
XLA Modules:
  0.0 604.0 jit_solution(7518295023820282792)
XLA Ops:
  11.4 4.6 copy.194
  16.3 7.8 %collective-permute-done = bf16[512,1024]{1,0:T(8,128)(2,1)S(1)} collective-permute-done((bf16[512,1024]{1,0:T(8,128)(2,1)}, bf16[512,1024]{1,0:T(8,128)(2,1)S(1)}, u32[]{:S(2)}, u32[]{:S(2)}) %collective-permute-start) | collective-permute-done | bytes 1048608 | tf_op jit(solution)/shard_map/ppermute | solution.py:81
  28.5 10.7 %collective-permute-done.1 = bf16[512,1024]{1,0:T(8,128)(2,1)} collective-permute-done((bf16[512,1024]{1,0:T(8,128)(2,1)S(1)}, bf16[512,1024]{1,0:T(8,128)(2,1)}, u32[]{:S(2)}, u32[]{:S(2)}) %collective-permute-start.1) | collective-permute-done | bytes 1048608 | tf_op jit(solution)/shard_map/ppermute | solution.py:81
  46.2 8.5 %collective-permute-done.2 = bf16[512,1024]{1,0:T(8,128)(2,1)} collective-permute-done((bf16[512,1024]{1,0:T(8,128)(2,1)}, bf16[512,1024]{1,0:T(8,128)(2,1)}, u32[]{:S(2)}, u32[]{:S(2)}) %collective-permute-start.2) | collective-permute-done | bytes 1048608 | tf_op jit(solution)/shard_map/ppermute | solution.py:81
  63.5 9.8 %all_gather.19 = bf16[8,64,16]{1,2,0:T(8,128)(2,1)S(1)} all-gather(bf16[1,64,16]{1,2,0:T(8,128)(2,1)S(1)} %get-tuple-element.366), channel_id=1, replica_groups=mesh['ctx'=8,'grp'=4] {'ctx'}, dimensions={0}, use_global_device_ids=true | all-gather | bytes 18432 | tf_op jit(solution)/shard_map/all_gather | solution.py:10
  73.4 9.8 %all_gather.20 = bf16[8,64,16,16]{1,3,2,0:T(8,128)(2,1)S(1)} all-gather(bf16[1,64,16,16]{1,3,2,0:T(8,128)(2,1)S(1)} %copy.209), channel_id=1, replica_groups=mesh['ctx'=8,'grp'=4] {'ctx'}, dimensions={0}, use_global_device_ids=true | all-gather | bytes 294912 | tf_op jit(solution)/shard_map/all_gather | solution.py:10
  91.6 54.4 %gather_fusion = f32[16384,64]{1,0:T(8,128)} fusion(f32[64,128]{0,1:T(8,128)S(1)} %copy.197, s32[16384]{0:T(1024)S(1)} %fusion.46), kind=kCustom, calls=%fused_computation | custom fusion | bytes 8454144 | tf_op jit(solution)/shard_map/jit(_take)/gather | solution.py:58
  146.7 9.9 %select_bitcast_fusion = f32[64,128,128]{0,2,1:T(8,128)} fusion(f32[128,128,64]{2,1,0:T(8,128)} %bitcast.218, pred[128,128]{1,0:T(8,128)(4,1)S(1)} %fusion.49), kind=kLoop, calls=%fused_computation.15 | loop fusion | flops 1048576 | bytes 8404992 | tf_op jit(solution)/shard_map/jit(_take)/select_n | solution.py:58
  156.6 7.4 %copy.198 = f32[64,128,128]{2,1,0:T(8,128)} copy(f32[64,128,128]{0,2,1:T(8,128)} %select_bitcast_fusion) | data formatting | bytes 8388608 | tf_op jit(solution)/shard_map/jit(_take)/select_n | solution.py:58
  164.0 10.1 %all_gather.22 = bf16[8,64,16]{1,2,0:T(8,128)(2,1)} all-gather(bf16[1,64,16]{1,2,0:T(8,128)(2,1)S(1)} %copy-done.39), channel_id=1, replica_groups=mesh['ctx'=8,'grp'=4] {'ctx'}, dimensions={0}, use_global_device_ids=true | all-gather | bytes 18432 | tf_op jit(solution)/shard_map/all_gather | solution.py:10
  180.7 10.1 %collective-permute-done.6 = bf16[512,1024]{1,0:T(8,128)(2,1)S(1)} collective-permute-done((bf16[512,1024]{1,0:T(8,128)(2,1)}, bf16[512,1024]{1,0:T(8,128)(2,1)S(1)}, u32[]{:S(2)}, u32[]{:S(2)}) %collective-permute-start.6) | collective-permute-done | bytes 1048608 | tf_op jit(solution)/shard_map/ppermute | solution.py:81
  220.1 13.3 %fusion.10 = f32[1024,1024]{1,0:T(8,128)S(1)} fusion(bf16[1024,4096]{1,0:T(8,128)(2,1)} %all-gather.2.cloned.1.call-done, bf16[8192,1024]{1,0:T(8,128)(2,1)} %constant_dynamic-update-slice_fusion, s32[]{:T(128)S(6)} %select_n.94), kind=kOutput, calls=%fused_computation.18 | convolution fusion | flops 8589934592 | bytes 20971524 | tf_op jit(solution)/shard_map/dot_general | solution.py:99
  236.4 7.0 %fusion.13 = f32[8,64,16,16]{3,2,1,0:T(8,128)S(1)} fusion(f32[8,128,64,16]{1,0,3,2:T(8,128)S(1)} %bitcast.214, f32[8,128]{1,0:T(8,128)S(1)} %get-tuple-element.384, f32[64,16,128]{2,1,0:T(8,128)S(1)} %get-tuple-element.370), kind=kOutput, calls=%fused_computation.21 | convolution fusion | flops 202375168 | bytes 5246976 | tf_op jit(solution)/shard_map/bgnt,btgc->bgcn/dot_general | solution.py:103
  249.5 10.8 %all_gather.23 = bf16[8,64,16,16]{1,3,2,0:T(8,128)(2,1)} all-gather(bf16[1,64,16,16]{1,3,2,0:T(8,128)(2,1)} %copy.225), channel_id=1, replica_groups=mesh['ctx'=8,'grp'=4] {'ctx'}, dimensions={0}, use_global_device_ids=true | all-gather | bytes 294912 | tf_op jit(solution)/shard_map/all_gather | solution.py:10
  260.3 13.0 %while.31 = (s32[]{:T(128)}, f32[64,16,16]{0,2,1:T(8,128)S(1)}, s32[]{:T(128)}, bf16[8,64,16]{1,2,0:T(8,128)(2,1)}, bf16[8,64,16,16]{1,3,2,0:T(8,128)(2,1)}, /*index=5*/s32[]{:T(128)}, s32[]{:T(128)}, s32[]{:T(128)}, s32[]{:T(128)}) while((s32[]{:T(128)}, f32[64,16,16]{0,2,1:T(8,128)S(1)}, s32[]{:T(128)}, ...), condition=%wide.region_8.9_spmd.clone, body=%wide.region_7.8_spmd.clone.sunk | while | flops 82952 | bytes 174247 | solution.py:28
  284.4 5.2 fusion.15
  289.6 28.8 %fusion.2 = f32[8,64,16,128]{3,2,1,0:T(8,128)S(1)} fusion(f32[8,128,128]{2,1,0:T(8,128)S(1)} %copy-done.13, f32[64,128,128]{2,1,0:T(8,128)S(1)} %copy-done, f32[8,128,64,16]{1,0,3,2:T(8,128)S(1)} %bitcast.215), kind=kOutput, calls=%fused_computation.7 | convolution fusion | flops 1619001344 | bytes 13107200 | tf_op jit(solution)/shard_map/bgts,btgc->bsgc/dot_general | solution.py:102
  318.4 26.4 %add_bitcast_fusion.1 = f32[8,128,64,16]{1,3,2,0:T(8,128)S(1)} fusion(f32[8,64,16,128]{3,2,1,0:T(8,128)S(1)} %fusion.15, f32[8,128,128]{2,1,0:T(8,128)S(1)} %copy-done.14, f32[64,128,128]{2,1,0:T(8,128)S(1)} %copy-done, bf16[8,128,64,16]{1,0,3,2:T(8,128)(2,1)S(1)} %bitcast.217), kind=kOutput, calls=%fused_computation.43 | convolution fusion | flops 1620049920 | bytes 15204352 | tf_op jit(solution)/shard_map/bgts,bsgc->btgc/dot_general | solution.py:86
  347.4 5.0 add_bitcast_fusion
  355.3 7.1 %fusion.22 = (bf16[1024,1024]{0,1:T(8,128)(2,1)}, bf16[1024,1024]{0,1:T(8,128)(2,1)}, bf16[1024,1024]{0,1:T(8,128)(2,1)}, bf16[1024,1024]{0,1:T(8,128)(2,1)S(1)}) fusion(bf16[1024,1024]{0,1:T(8,128)(2,1)S(1)} %copy-done.6, bf16[1024,1024]{0,1:T(8,128)(2,1)S(1)} %copy-done.9, f32[1024,1024]{1,0:T(8,128)S(1)} %copy-done.11, f32[1024]{0:T(1024)S(1)} %copy-done.42, ...), kind=kLoop, calls=%fused_computation.35 | loop fusion | flops 19922944 | bytes 27267072 | tf_op jit(solution)/shard_map/convert_element_type | solution.py:126
  363.7 14.2 %convert_bitcast_fusion = bf16[4096,1024]{0,1:T(8,128)(2,1)} fusion(bf16[1024,1024]{0,1:T(8,128)(2,1)S(1)} %get-tuple-element.359, bf16[1024,4096]{1,0:T(8,128)(2,1)} %all-gather.2.cloned.1.call-done), kind=kOutput, calls=%fused_computation.16 | convolution fusion | flops 8594128896 | bytes 18874368 | tf_op jit(solution)/shard_map/dot_general | solution.py:127
  379.5 14.6 %convolution_convert_fusion = bf16[1024,4096]{1,0:T(8,128)(2,1)} fusion(bf16[1024,1024]{0,1:T(8,128)(2,1)S(1)} %copy-done.28, bf16[8192,1024]{1,0:T(8,128)(2,1)} %constant_dynamic-update-slice_fusion, s32[]{:T(128)S(6)} %select_n.94), kind=kOutput, calls=%fused_computation.17 | convolution fusion | flops 8594128896 | bytes 18874372 | tf_op jit(solution)/shard_map/dot_general | solution.py:117
  404.7 45.0 %reduce-scatter.5.cloned.1.call-done = bf16[512,1024]{0,1:T(8,128)(2,1)} async-done(((bf16[4096,1024]{0,1:T(8,128)(2,1)}), bf16[512,1024]{0,1:T(8,128)(2,1)}) %reduce-scatter.5.cloned.1.call-update) | async-done | bytes 1048592 | tf_op jit(solution)/shard_map/reduce_scatter | solution.py:130
  452.2 145.0 %reduce-scatter.3.cloned.1.call-done = bf16[1024,1024]{1,0:T(8,128)(2,1)} async-done(((bf16[1024,4096]{1,0:T(8,128)(2,1)}), bf16[1024,1024]{1,0:T(8,128)(2,1)}) %reduce-scatter.3.cloned.1.call-update) | async-done | bytes 2097168 | tf_op jit(solution)/shard_map/reduce_scatter | solution.py:121
  (227 shorter events, 124.2 us)
Async XLA Ops:
  7.2 212.9 %all-gather.2.cloned.1.call-start = ((), (), s32[]{:S(2)}) async-start(), calls=%async_computation.3 | async-start | bytes 10485760 | tf_op jit(solution)/shard_map/all_gather | solution.py:98
  7.9 441.8 %reduce-scatter.5.cloned.1.call-start = ((), (), s32[]{:S(2)}) async-start(), calls=%async_computation.4 | async-start | bytes 9437184 | tf_op jit(solution)/shard_map/reduce_scatter | solution.py:130
  7.9 16.1 %collective-permute-start = (bf16[512,1024]{1,0:T(8,128)(2,1)}, bf16[512,1024]{1,0:T(8,128)(2,1)S(1)}, u32[]{:S(2)}, u32[]{:S(2)}) collective-permute-start(bf16[512,1024]{1,0:T(8,128)(2,1)} %param.19), channel_id=1, source_target_pairs={{0,4},{4,8},{8,12},{12,16},{16,20},{20,24},{24,28},{28,0},{1,5},{5... | collective-permute-start | bytes 3145736 | tf_op jit(solution)/shard_map/ppermute | solution.py:81
  8.5 15.9 %copy-start.40 = (f32[64,16]{0,1:T(8,128)S(1)}, f32[64,16]{0,1:T(8,128)}, u32[]{:S(2)}) copy-start(f32[64,16]{0,1:T(8,128)} %param.16) | copy-start | bytes 12292
  8.5 15.9 %copy-start.41 = (f32[64,16]{0,1:T(8,128)S(1)}, f32[64,16]{0,1:T(8,128)}, u32[]{:S(2)}) copy-start(f32[64,16]{0,1:T(8,128)} %param.17) | copy-start | bytes 12292
  11.4 17.2 %copy-start.5 = (bf16[1024,1024]{0,1:T(8,128)(2,1)}, bf16[1024,1024]{0,1:T(8,128)(2,1)S(1)}, u32[]{:S(2)}) copy-start(bf16[1024,1024]{0,1:T(8,128)(2,1)S(1)} %copy.193) | copy-start | bytes 6291460
  24.0 18.9 %copy-start.25 = (bf16[512,1024]{1,0:T(8,128)(2,1)}, bf16[512,1024]{1,0:T(8,128)(2,1)S(1)}, u32[]{:S(2)}) copy-start(bf16[512,1024]{1,0:T(8,128)(2,1)S(1)} %collective-permute-done) | copy-start | bytes 3145732
  24.0 15.2 %collective-permute-start.1 = (bf16[512,1024]{1,0:T(8,128)(2,1)S(1)}, bf16[512,1024]{1,0:T(8,128)(2,1)}, u32[]{:S(2)}, u32[]{:S(2)}) collective-permute-start(bf16[512,1024]{1,0:T(8,128)(2,1)S(1)} %collective-permute-done), channel_id=1, source_target_pairs={{0,4},{4,8},{8,12},{12,16},{16,20},{20,24},{24,28},{28,0},{1,5},{5... | collective-permute-start | bytes 3145736 | tf_op jit(solution)/shard_map/ppermute | solution.py:81
  24.2 18.7 %copy-start.43 = (s32[8]{0:T(128)}, s32[8]{0:T(128)S(1)}, u32[]{:S(2)}) copy-start(s32[8]{0:T(128)S(1)} %slice_reduce_fusion) | copy-start | bytes 100
  24.3 18.6 %copy-start.44 = (s32[8]{0:T(128)}, s32[8]{0:T(128)S(1)}, u32[]{:S(2)}) copy-start(s32[8]{0:T(128)S(1)} %slice_reduce_fusion.1) | copy-start | bytes 100
  39.3 15.4 %collective-permute-start.2 = (bf16[512,1024]{1,0:T(8,128)(2,1)}, bf16[512,1024]{1,0:T(8,128)(2,1)}, u32[]{:S(2)}, u32[]{:S(2)}) collective-permute-start(bf16[512,1024]{1,0:T(8,128)(2,1)} %collective-permute-done.1), channel_id=1, source_target_pairs={{0,4},{4,8},{8,12},{12,16},{16,20},{20,24},{24,28},{28,0},{1,5},{5... | collective-permute-start | bytes 3145736 | tf_op jit(solution)/shard_map/ppermute | solution.py:81
  43.8 19.4 %copy-start.31 = (f32[64,16]{1,0:T(8,128)}, f32[64,16]{1,0:T(8,128)S(1)}, u32[]{:S(2)}) copy-start(f32[64,16]{1,0:T(8,128)S(1)} %copy.204) | copy-start | bytes 12292
  43.9 19.3 %copy-start.33 = (f32[64,16]{1,0:T(8,128)}, f32[64,16]{1,0:T(8,128)S(1)}, u32[]{:S(2)}) copy-start(f32[64,16]{1,0:T(8,128)S(1)} %copy.206) | copy-start | bytes 12292
  44.6 18.6 %copy-start.29 = (f32[64,16]{1,0:T(8,128)}, f32[64,16]{1,0:T(8,128)S(1)}, u32[]{:S(2)}) copy-start(f32[64,16]{1,0:T(8,128)S(1)} %copy.201) | copy-start | bytes 12292
  44.7 18.5 %copy-start.35 = (f32[64,16]{1,0:T(8,128)}, f32[64,16]{1,0:T(8,128)S(1)}, u32[]{:S(2)}) copy-start(f32[64,16]{1,0:T(8,128)S(1)} %copy.202) | copy-start | bytes 12292
  44.8 18.5 %copy-start.37 = (f32[64,16]{1,0:T(8,128)}, f32[64,16]{1,0:T(8,128)S(1)}, u32[]{:S(2)}) copy-start(f32[64,16]{1,0:T(8,128)S(1)} %copy.200) | copy-start | bytes 12292
  54.7 28.5 %collective-permute-start.3 = (bf16[512,1024]{1,0:T(8,128)(2,1)}, bf16[512,1024]{1,0:T(8,128)(2,1)}, u32[]{:S(2)}, u32[]{:S(2)}) collective-permute-start(bf16[512,1024]{1,0:T(8,128)(2,1)} %collective-permute-done.2), channel_id=1, source_target_pairs={{0,4},{4,8},{8,12},{12,16},{16,20},{20,24},{24,28},{28,0},{1,5},{5... | collective-permute-start | bytes 3145736 | tf_op jit(solution)/shard_map/ppermute | solution.py:81
  83.2 62.9 %collective-permute-start.4 = (bf16[512,1024]{1,0:T(8,128)(2,1)}, bf16[512,1024]{1,0:T(8,128)(2,1)}, u32[]{:S(2)}, u32[]{:S(2)}) collective-permute-start(bf16[512,1024]{1,0:T(8,128)(2,1)} %collective-permute-done.3), channel_id=1, source_target_pairs={{0,4},{4,8},{8,12},{12,16},{16,20},{20,24},{24,28},{28,0},{1,5},{5... | collective-permute-start | bytes 3145736 | tf_op jit(solution)/shard_map/ppermute | solution.py:81
  146.1 29.1 %collective-permute-start.5 = (bf16[512,1024]{1,0:T(8,128)(2,1)}, bf16[512,1024]{1,0:T(8,128)(2,1)}, u32[]{:S(2)}, u32[]{:S(2)}) collective-permute-start(bf16[512,1024]{1,0:T(8,128)(2,1)} %collective-permute-done.4), channel_id=1, source_target_pairs={{0,4},{4,8},{8,12},{12,16},{16,20},{20,24},{24,28},{28,0},{1,5},{5... | collective-permute-start | bytes 3145736 | tf_op jit(solution)/shard_map/ppermute | solution.py:81
  156.6 20.3 %copy-start.34 = (f32[64,16]{1,0:T(8,128)S(1)}, f32[64,16]{1,0:T(8,128)}, u32[]{:S(2)}) copy-start(f32[64,16]{1,0:T(8,128)} %copy-done.33) | copy-start | bytes 12292
  175.2 15.6 %collective-permute-start.6 = (bf16[512,1024]{1,0:T(8,128)(2,1)}, bf16[512,1024]{1,0:T(8,128)(2,1)S(1)}, u32[]{:S(2)}, u32[]{:S(2)}) collective-permute-start(bf16[512,1024]{1,0:T(8,128)(2,1)} %collective-permute-done.5), channel_id=1, source_target_pairs={{0,4},{4,8},{8,12},{12,16},{16,20},{20,24},{24,28},{28,0},{1,5},{5... | collective-permute-start | bytes 3145736 | tf_op jit(solution)/shard_map/ppermute | solution.py:81
  180.7 32.7 %copy-start.17 = (f32[8,64,16,16]{3,2,1,0:T(8,128)}, f32[8,64,16,16]{3,2,1,0:T(8,128)S(1)}, u32[]{:S(2)}) copy-start(f32[8,64,16,16]{3,2,1,0:T(8,128)S(1)} %get-tuple-element.352) | copy-start | bytes 1572868
  289.6 28.8 %copy-start.14 = (f32[8,128,128]{2,1,0:T(8,128)S(1)}, f32[8,128,128]{2,1,0:T(8,128)}, u32[]{:S(2)}) copy-start(f32[8,128,128]{2,1,0:T(8,128)} %and_convert_fusion) | copy-start | bytes 1572868
  377.9 219.3 %reduce-scatter.3.cloned.1.call-start = ((), (), s32[]{:S(2)}) async-start(), calls=%async_computation.2 | async-start | bytes 10485760 | tf_op jit(solution)/shard_map/reduce_scatter | solution.py:121
  (32 other events, 165.7 us)
Sparse Core Ops, SparseCore 0:
  9.6 152.3 all-gather.1
  378.1 71.5 reduce-scatter.4
  452.7 144.4 reduce-scatter.2
